TPU v7x, 32 devices: a whole 2x2x4 slice. The times are simulated.
32 devices in a mesh: groups: 2 (over x), expert: 16 (over z, y, core).
Axes of the slice: x: 2, y: 2, z: 4, core: 2. Of those that a mesh axis runs over, the one named last changes fastest.
Arguments:
- tokens: bfloat16 [2048, 2048], P(('groups', 'expert')), parts along dimension 0, may hold values from -6 to 6
- expert_ids: int32 [2048, 8], P(('groups', 'expert')), parts along dimension 0, may hold values from 0 to 15, as said below
- gate_weights: float32 [2048, 8], P(('groups', 'expert')), parts along dimension 0, may hold values from 0.05 to 0.5
- w_gate: bfloat16 [16, 2048, 768], P('expert'), may hold values from -0.125 to 0.125
- w_up: bfloat16 [16, 2048, 768], P('expert'), may hold values from -0.125 to 0.125
- w_down: bfloat16 [16, 768, 2048], P('expert'), may hold values from -0.21875 to 0.21875
Outputs:
- mixed: bfloat16 [2048, 2048], P(('groups', 'expert')), parts along dimension 0
There are 2 independent parts, one for each index of `groups`. A program takes and returns all parts, laid end to end along the dimension named above; an argument that names none is the same for every part. Nothing has to cross between parts.
Inputs may be any that keep to these rules, and one draw needn't show every extreme that they name: `expert_ids`: each token names 8 different experts. Exactly 2 experts are named exactly 64 times by the tokens of every device; every other expert is named at most 28 times by the tokens of one device, and in every draw some such expert is named exactly 28 times by the tokens of every device.
All inputs are finite; a program needn't handle non-finite values.
Results may differ from a plain program's by a relative error of at most 0.0057.
Values may be sent and summed in bfloat16 or wider, within the bound.
A program may use at most 128 MiB of HBM per device.

v0:
```python
import jax
import jax.numpy as jnp
from jax import lax
from jax.sharding import PartitionSpec as P

row_block = 256


def swiglu_rows(rows_in, weights):
    gate_part = jnp.dot(rows_in, weights[0], preferred_element_type=jnp.float32)
    up_part = jnp.dot(rows_in, weights[1], preferred_element_type=jnp.float32)
    hidden = (jax.nn.silu(gate_part) * up_part).astype(jnp.bfloat16)
    return jnp.dot(hidden, weights[2], preferred_element_type=jnp.float32).astype(jnp.bfloat16)


def run_blocks(source_rows, block_total, weights, results):

    def block_step(block_num, current):
        row_start = block_num * row_block
        rows_in = lax.dynamic_slice_in_dim(source_rows, row_start, row_block, 0)
        return lax.dynamic_update_slice_in_dim(current, swiglu_rows(rows_in, weights), row_start, 0)

    return lax.fori_loop(jnp.zeros((), jnp.int32), block_total, block_step, results)


def route_and_run(tokens, flat_ids, slot_rank, routed, capacity, device_count, own_weights):
    local_tokens, model_width = tokens.shape
    slot_total = flat_ids.shape[0]
    top_count = slot_total // local_tokens
    buffer_rows = device_count * capacity
    padded_rows = (buffer_rows + row_block - 1) // row_block * row_block
    send_slot = jnp.where(routed, flat_ids * capacity + slot_rank, buffer_rows)
    token_of_slot = jnp.arange(slot_total, dtype=jnp.int32) // top_count
    source_row = jnp.zeros((buffer_rows,), jnp.int32).at[send_slot].set(token_of_slot, mode="drop")
    slot_filled = jnp.zeros((buffer_rows,), jnp.int32).at[send_slot].set(1, mode="drop")
    send_counts = jnp.sum(slot_filled.reshape(device_count, capacity), axis=1)
    outgoing = jnp.where(slot_filled[:, None] > 0, tokens[source_row], jnp.zeros((), jnp.bfloat16))
    outgoing = outgoing.reshape(device_count, capacity, model_width)
    count_column = send_counts.astype(jnp.bfloat16).reshape(device_count, 1)
    incoming, arrived = (
        lax.all_to_all(outgoing, "expert", split_axis=0, concat_axis=0, tiled=True),
        lax.all_to_all(count_column, "expert", split_axis=0, concat_axis=0, tiled=True),
    )
    arrived_counts = arrived.reshape(-1).astype(jnp.int32)
    offsets = jnp.cumsum(arrived_counts) - arrived_counts
    live_total = jnp.sum(arrived_counts)
    slot_index = jnp.arange(buffer_rows, dtype=jnp.int32)
    source_of = slot_index // capacity
    within = slot_index % capacity
    is_live = within < arrived_counts[source_of]
    packed_pos = offsets[source_of] + within
    target_pos = jnp.where(is_live, packed_pos, padded_rows)
    compact_source = (
        jnp.full((padded_rows,), buffer_rows, jnp.int32).at[target_pos].set(slot_index, mode="drop")
    )
    flat_incoming = jnp.concatenate(
        [incoming.reshape(buffer_rows, model_width), jnp.zeros((1, model_width), jnp.bfloat16)],
        axis=0,
    )
    compact = flat_incoming[compact_source]
    block_need = (live_total + row_block - 1) // row_block
    results = run_blocks(
        compact, block_need, own_weights, jnp.zeros((padded_rows, model_width), jnp.bfloat16)
    )
    back_slots = results[jnp.where(is_live, packed_pos, 0)]
    back_slots = jnp.where(is_live[:, None], back_slots, jnp.zeros((), jnp.bfloat16))
    back_slots = back_slots.reshape(device_count, capacity, model_width)
    returned_rows = lax.all_to_all(back_slots, "expert", split_axis=0, concat_axis=0, tiled=True)
    picked = returned_rows.reshape(buffer_rows, model_width)[jnp.where(routed, send_slot, 0)]
    return jnp.where(routed[:, None], picked, jnp.zeros((), jnp.bfloat16))


def shards(tokens, expert_ids, gate_weights, w_gate, w_up, w_down):
    device_count = lax.axis_size("expert")
    local_tokens, model_width = tokens.shape
    top_count = expert_ids.shape[1]
    expert_total = device_count * w_gate.shape[0]
    capacity = min(
        local_tokens, 4 * ((local_tokens * top_count + expert_total - 1) // expert_total)
    )
    flat_ids = expert_ids.reshape(-1)
    slot_total = flat_ids.shape[0]
    expert_range = jnp.arange(device_count, dtype=jnp.int32)
    onehot = (flat_ids[:, None] == expert_range[None, :]).astype(jnp.int32)
    slot_rank = jnp.sum(jnp.cumsum(onehot, axis=0) * onehot, axis=1) - 1
    own_weights = (w_gate[0], w_up[0], w_down[0])
    routed = jnp.ones((slot_total,), jnp.bool_)
    slot_values = route_and_run(
        tokens, flat_ids, slot_rank, routed, capacity, device_count, own_weights
    )
    picked = slot_values.reshape(local_tokens, top_count, model_width)
    mixed = jnp.sum(picked.astype(jnp.float32) * gate_weights[:, :, None], axis=1)
    return mixed.astype(jnp.bfloat16)


def solution(mesh):
    placed = (
        P(("groups", "expert"), None),
        P(("groups", "expert"), None),
        P(("groups", "expert"), None),
        P("expert", None, None),
        P("expert", None, None),
        P("expert", None, None),
    )
    return jax.shard_map(
        shards, mesh=mesh, in_specs=placed, out_specs=P(("groups", "expert"), None), check_vma=False
    )
```

profile of v0, /device:TPU:15, one launch (start us, length us, event | category | flops | bytes accessed | tf_op | source)
XLA Modules:
  0.0 305.7 jit_solution(18314291863465316378)
XLA Ops:
  0.0 0.0 copy-start
  0.0 0.8 copy.30
  0.8 0.1 eq.31
  0.9 0.1 eq.27
  1.0 0.7 broadcast_multiply_fusion
  1.7 1.1 reduce-window.19
  2.8 0.2 slice_reduce_fusion
  3.1 0.1 fusion.14
  3.2 0.1 copy.29
  3.3 0.1 mul.40
  3.4 2.4 scatter_custom_fusion
  5.9 0.1 reshape.244
  5.9 0.1 reduce_sum.37
  6.1 0.7 copy.33
  6.8 6.5 %all-to-all-start = ((bf16[16,1,1]{2,1,0:T(2,128)(2,1)}), bf16[16,1,1]{2,1,0:T(2,128)(2,1)S(1)}, u32[]{:S(2)}, u32[]{:S(2)}) async-start(bf16[16,1,1]{2,1,0:T(2,128)(2,1)} %copy.33), calls=%async_computation | async-start | bytes 16384 | tf_op jit(solution)/shard_map/all_to_all | solution.py:42
  13.3 0.1 broadcast_in_dim.61
  13.4 2.4 scatter_custom_fusion.1
  15.9 6.0 %gather_fusion = bf16[1024,2048]{1,0:T(8,128)(2,1)} fusion(bf16[64,2048]{1,0:T(8,128)(2,1)S(1)} %copy-done, s32[1024]{0:T(1024)S(1)} %fusion.20), kind=kCustom, calls=%fused_computation | custom fusion | bytes 8392704 | tf_op jit(solution)/shard_map/gather | solution.py:37
  21.9 4.5 %broadcast_select_fusion = bf16[16,64,2048]{2,1,0:T(8,128)(2,1)} fusion(bf16[16,64,2048]{2,1,0:T(8,128)(2,1)} %bitcast.78, pred[16,64]{1,0:T(8,128)(4,1)S(1)} %broadcast_in_dim.61), kind=kLoop, calls=%fused_computation.20 | loop fusion | flops 2097152 | bytes 8389632 | tf_op jit(solution)/shard_map/jit(_where)/select_n | solution.py:37
  26.4 0.0 all-to-all-done
  26.4 6.0 %all-to-all-start.1 = ((bf16[16,64,2048]{2,1,0:T(8,128)(2,1)}), bf16[16,64,2048]{2,1,0:T(8,128)(2,1)}, u32[]{:S(2)}, u32[]{:S(2)}) async-start(bf16[16,64,2048]{2,1,0:T(8,128)(2,1)} %broadcast_select_fusion), calls=%async_computation.1 | async-start | bytes 8388608 | tf_op jit(solution)/shard_map/all_to_all | solution.py:41
  32.7 0.9 convert_reduce_fusion.1
  34.3 0.1 reduce.11
  34.4 0.6 fusion.33
  35.1 4.2 %compare_select_fusion.6 = s32[1024,1]{0,1:T(1,128)S(1)} fusion(s32[]{:T(128)} %bitcast.13, s32[]{:T(128)} %bitcast.14, s32[]{:T(128)} %bitcast.15, s32[]{:T(128)} %bitcast.16, s32[]{:T(128)} %bitcast.17, s32[]{:T(128)} %bitcast.19, s32[]{:T(128)} %bitcast.18), kind=kLoop, calls=%fused_computation.48 | loop fusion | flops 23552 | bytes 4124 | tf_op jit(solution)/shard_map/gather | solution.py:50
  39.3 5.7 %select_select_fusion.1 = s32[1024]{0:T(1024)S(1)} fusion(pred[1024]{0:T(1024)(128)(4,1)S(1)} %compare_reduce_fusion, pred[1024]{0:T(1024)(128)(4,1)S(1)} %compare_reduce_fusion.1, pred[1024]{0:T(1024)(128)(4,1)S(1)} %compare_reduce_fusion.2, pred[1024]{0:T(1024)(128)(4,1)S(1)} %compare_reduce_fusion.3, pred[1024]{0:T(1024)(128)(4,1)S(1)} %compare_reduce_fusion.4, ...), kind=kLoop, calls=%fused_computation.72 | loop fusion | flops 9216 | bytes 17444 | tf_op jit(solution)/shard_map/gather | solution.py:50
  45.0 0.1 gather.29
  45.1 0.7 fusion.34
  45.8 4.5 %compare_select_fusion.7 = s32[1024,1]{0,1:T(1,128)S(1)} fusion(s32[]{:T(128)} %bitcast.34, s32[]{:T(128)} %bitcast.35, s32[]{:T(128)} %bitcast.36, s32[]{:T(128)} %bitcast.37, s32[]{:T(128)} %bitcast.38, s32[]{:T(128)} %bitcast.40, s32[]{:T(128)} %bitcast.39), kind=kLoop, calls=%fused_computation.49 | loop fusion | flops 23552 | bytes 4124 | tf_op jit(solution)/shard_map/gather | solution.py:51
  50.3 5.4 %select_select_fusion = s32[1024]{0:T(1024)S(1)} fusion(pred[1024]{0:T(1024)(128)(4,1)S(1)} %compare_reduce_fusion, pred[1024]{0:T(1024)(128)(4,1)S(1)} %compare_reduce_fusion.1, pred[1024]{0:T(1024)(128)(4,1)S(1)} %compare_reduce_fusion.2, pred[1024]{0:T(1024)(128)(4,1)S(1)} %compare_reduce_fusion.3, pred[1024]{0:T(1024)(128)(4,1)S(1)} %compare_reduce_fusion.4, ...), kind=kLoop, calls=%fused_computation.71 | loop fusion | flops 9216 | bytes 17444 | tf_op jit(solution)/shard_map/gather | solution.py:51
  55.8 4.3 %scatter_custom_fusion.2 = s32[1024]{0:T(1024)S(1)} fusion(s32[1024]{0:T(1024)S(1)} %bitcast.89, s32[1024]{0:T(1024)S(1)} %iota.46, s32[]{:T(128)} %constant.94.clone.1), kind=kCustom, calls=%fused_computation.80 | custom fusion | bytes 4100 | tf_op jit(solution)/shard_map/scatter | solution.py:54
  60.2 64.7 %all-to-all-done.1 = bf16[16,64,2048]{2,1,0:T(8,128)(2,1)} async-done(((bf16[16,64,2048]{2,1,0:T(8,128)(2,1)}), bf16[16,64,2048]{2,1,0:T(8,128)(2,1)}, u32[]{:S(2)}, u32[]{:S(2)}) %all-to-all-start.1) | async-done | bytes 4194336 | tf_op jit(solution)/shard_map/all_to_all | solution.py:41
  124.8 4.7 %concatenate.3 = bf16[1025,2048]{1,0:T(8,128)(2,1)} pad(bf16[1024,2048]{1,0:T(8,128)(2,1)} %bitcast.22, bf16[]{:T(256)} %constant.98.clone.1), padding=0_1x0_0 | pad | bytes 8392706 | tf_op jit(solution)/shard_map/concatenate | solution.py:56
  129.6 11.6 %gather_fusion.1 = bf16[1024,2048]{1,0:T(8,128)(2,1)} fusion(bf16[1025,2048]{1,0:T(8,128)(2,1)} %concatenate.3, s32[1024]{0:T(1024)S(1)} %fusion.21), kind=kCustom, calls=%fused_computation.1 | custom fusion | bytes 8392704 | tf_op jit(solution)/shard_map/gather | solution.py:60
  141.1 2.5 broadcast_in_dim.60
  143.6 0.4 copy-done.2
  144.0 19.3 %while.10 = (s32[]{:T(128)}, bf16[1024,2048]{1,0:T(8,128)(2,1)}, s32[]{:T(128)}, bf16[1024,2048]{1,0:T(8,128)(2,1)}, bf16[2048,768]{1,0:T(8,128)(2,1)S(1)}, /*in...) while((s32[]{:T(128)}, bf16[1024,2048]{1,0:T(8,128)(2,1)}, ...), condition=%wide.region_10.11_spmd, body=%wide.region_9.10_spmd.sunk | while | flops 2417623040 | bytes 14156959 | solution.py:23
  144.0 3.1 %fusion.50 = f32[256,768]{1,0:T(8,128)} fusion(bf16[2048,768]{1,0:T(8,128)(2,1)S(1)} %get-tuple-element.164, bf16[1024,2048]{1,0:T(8,128)(2,1)} %get-tuple-element.163, s32[]{:T(128)S(6)} %select_n.234), kind=kOutput, calls=%fused_computation.12.clone.1 | convolution fusion | flops 805306368 | bytes 4980740 | tf_op jit(solution)/shard_map/while/body/dot_general | solution.py:10
  147.2 6.6 %fusion.51 = bf16[1024,2048]{1,0:T(8,128)(2,1)} fusion(bf16[1024,2048]{1,0:T(8,128)(2,1)} %get-tuple-element.150, s32[]{:T(128)S(6)} %select_n.234, bf16[768,2048]{1,0:T(8,128)(2,1)} %get-tuple-element.166, bf16[2048,768]{1,0:T(8,128)(2,1)} %get-tuple-element.165, bf16[1024,2048]{1,0:T(8,128)(2,1)} %get-tuple-element.163, f32[256,768]{1,0:T(8,128)} %fusion.50), kind=kOutput, calls=%fused_computation.8.clone.1 | convolution fusion | flops 1612316672 | bytes 9176064 | tf_op jit(solution)/shard_map/while/body/dot_general | solution.py:13
  153.7 3.1 %fusion.50 = f32[256,768]{1,0:T(8,128)} fusion(bf16[2048,768]{1,0:T(8,128)(2,1)S(1)} %get-tuple-element.164, bf16[1024,2048]{1,0:T(8,128)(2,1)} %get-tuple-element.163, s32[]{:T(128)S(6)} %select_n.234), kind=kOutput, calls=%fused_computation.12.clone.1 | convolution fusion | flops 805306368 | bytes 4980740 | tf_op jit(solution)/shard_map/while/body/dot_general | solution.py:10
  156.8 6.5 %fusion.51 = bf16[1024,2048]{1,0:T(8,128)(2,1)} fusion(bf16[1024,2048]{1,0:T(8,128)(2,1)} %get-tuple-element.150, s32[]{:T(128)S(6)} %select_n.234, bf16[768,2048]{1,0:T(8,128)(2,1)} %get-tuple-element.166, bf16[2048,768]{1,0:T(8,128)(2,1)} %get-tuple-element.165, bf16[1024,2048]{1,0:T(8,128)(2,1)} %get-tuple-element.163, f32[256,768]{1,0:T(8,128)} %fusion.50), kind=kOutput, calls=%fused_computation.8.clone.1 | convolution fusion | flops 1612316672 | bytes 9176064 | tf_op jit(solution)/shard_map/while/body/dot_general | solution.py:13
  163.3 11.6 %gather_fusion.2 = bf16[1024,2048]{1,0:T(8,128)(2,1)} fusion(bf16[1024,2048]{1,0:T(8,128)(2,1)} %get-tuple-element.43, s32[1024]{0:T(1024)S(1)} %broadcast_clamp_fusion), kind=kCustom, calls=%fused_computation.2 | custom fusion | bytes 8392704 | tf_op jit(solution)/shard_map/gather | solution.py:65
  174.9 4.5 %broadcast_select_fusion.1 = bf16[16,64,2048]{2,1,0:T(8,128)(2,1)} fusion(bf16[16,64,2048]{2,1,0:T(8,128)(2,1)} %bitcast.77, pred[16,64]{1,0:T(8,128)(4,1)S(1)} %fusion.16), kind=kLoop, calls=%fused_computation.21 | loop fusion | flops 2097152 | bytes 8389632 | tf_op jit(solution)/shard_map/jit(_where)/select_n | solution.py:66
  179.4 24.2 %all-to-all-start.2 = ((bf16[16,64,2048]{2,1,0:T(8,128)(2,1)}), bf16[16,64,2048]{2,1,0:T(8,128)(2,1)}, u32[]{:S(2)}, u32[]{:S(2)}) async-start(bf16[16,64,2048]{2,1,0:T(8,128)(2,1)} %broadcast_select_fusion.1), calls=%async_computation.2 | async-start | bytes 8388608 | tf_op jit(solution)/shard_map/all_to_all | solution.py:68
  203.6 0.1 copy.35
  203.7 92.4 %all-to-all-done.2 = bf16[16,64,2048]{2,1,0:T(8,128)(2,1)} async-done(((bf16[16,64,2048]{2,1,0:T(8,128)(2,1)}), bf16[16,64,2048]{2,1,0:T(8,128)(2,1)}, u32[]{:S(2)}, u32[]{:S(2)}) %all-to-all-start.2) | async-done | bytes 4194336 | tf_op jit(solution)/shard_map/all_to_all | solution.py:68
  296.0 7.1 %gather_fusion.3 = bf16[512,2048]{1,0:T(8,128)(2,1)S(1)} fusion(bf16[1024,2048]{1,0:T(8,128)(2,1)} %bitcast.49, s32[1024]{0:T(1024)S(1)} %pad_clamp_fusion), kind=kCustom, calls=%fused_computation.3 | custom fusion | bytes 4196352 | tf_op jit(solution)/shard_map/gather | solution.py:69
  303.2 2.5 fusion.12
  (32 shorter events, 0.5 us)
Async XLA Ops:
  0.0 15.9 %copy-start = (bf16[64,2048]{1,0:T(8,128)(2,1)S(1)}, bf16[64,2048]{1,0:T(8,128)(2,1)}, u32[]{:S(2)}) copy-start(bf16[64,2048]{1,0:T(8,128)(2,1)} %param.8) | copy-start | bytes 786436
  6.8 19.6 %all-to-all-start = ((bf16[16,1,1]{2,1,0:T(2,128)(2,1)}), bf16[16,1,1]{2,1,0:T(2,128)(2,1)S(1)}, u32[]{:S(2)}, u32[]{:S(2)}) async-start(bf16[16,1,1]{2,1,0:T(2,128)(2,1)} %copy.33), calls=%async_computation | async-start | bytes 16384 | tf_op jit(solution)/shard_map/all_to_all | solution.py:42
  26.4 98.5 %all-to-all-start.1 = ((bf16[16,64,2048]{2,1,0:T(8,128)(2,1)}), bf16[16,64,2048]{2,1,0:T(8,128)(2,1)}, u32[]{:S(2)}, u32[]{:S(2)}) async-start(bf16[16,64,2048]{2,1,0:T(8,128)(2,1)} %broadcast_select_fusion), calls=%async_computation.1 | async-start | bytes 8388608 | tf_op jit(solution)/shard_map/all_to_all | solution.py:41
  141.1 2.9 copy-start.2
  179.4 24.2 %copy-start.1 = (f32[64,8]{0,1:T(8,128)S(1)}, f32[64,8]{0,1:T(8,128)}, u32[]{:S(2)}) copy-start(f32[64,8]{0,1:T(8,128)} %param.10) | copy-start | bytes 6148
  179.4 116.6 %all-to-all-start.2 = ((bf16[16,64,2048]{2,1,0:T(8,128)(2,1)}), bf16[16,64,2048]{2,1,0:T(8,128)(2,1)}, u32[]{:S(2)}, u32[]{:S(2)}) async-start(bf16[16,64,2048]{2,1,0:T(8,128)(2,1)} %broadcast_select_fusion.1), calls=%async_computation.2 | async-start | bytes 8388608 | tf_op jit(solution)/shard_map/all_to_all | solution.py:68
where the time goes:
time: 307 us; the launch traced here: 306 us
  waiting for transfers between devices  157 us (51%)
  local copies, waits for them, and re-layouts  56.8 us (19%)
  starting transfers between devices  36.7 us (12%)
  other arithmetic  35 us (11%)
  matrix products  19.3 us (6%)
    all_to_all x1, waiting for transfers between devices, route_and_run(): lax.all_to_all(back_slots, 'expert', split_axis=0, concat_axis=0, tiled=T...  92.4 us
    all_to_all x1, waiting for transfers between devices, route_and_run(): lax.all_to_all(outgoing, 'expert', split_axis=0, concat_axis=0, tiled=True)  64.7 us
    all_to_all x1, starting transfers between devices, route_and_run(): lax.all_to_all(back_slots, 'expert', split_axis=0, concat_axis=0, tiled=T...  24.2 us
    dot_general x2, matrix products, swiglu_rows(): jnp.dot(hidden, weights[2], preferred_element_type=jnp.float32)  13.1 us
    gather x1, local copies, waits for them, and re-layouts, route_and_run(): compact = flat_incoming[compact_source]  11.6 us
    gather x1, local copies, waits for them, and re-layouts, route_and_run(): back_slots = results[jnp.where(is_live, packed_pos, 0)]  11.6 us
    gather x11, other arithmetic, route_and_run(): is_live = within < arrived_counts[source_of]  10.2 us
    gather x2, other arithmetic, route_and_run(): packed_pos = offsets[source_of] + within  9.94 us
  transfers between devices with their start and end apart: 3, of which 2 were waited for; matrix products, arithmetic and copies ran while one was open for 13% of the time, Pallas kernels for 0%

commit v1 on v0

--- a/solution.py
+++ b/solution.py
@@ -4,6 +4,29 @@
 from jax.sharding import PartitionSpec as P
 
 row_block = 256
+
+
+def cut_along(x, dim, devices):
+    lengths = x.shape
+    tiles = x.reshape(*lengths[:dim], devices, lengths[dim] // devices, *lengths[dim + 1 :])
+    return jnp.moveaxis(tiles, dim, 0)
+
+
+def in_order(tiles, dim):
+    shape = list(tiles.shape[1:])
+    shape[dim] *= tiles.shape[0]
+    return jnp.moveaxis(tiles, 0, dim).reshape(shape)
+
+
+def rotated_exchange(x, axis, split_dim, concat_dim):
+    length, index = (lax.axis_size(axis), lax.axis_index(axis))
+    blocks = cut_along(x, split_dim, length)
+    done = [blocks[index]]
+    for step in range(1, length):
+        sent = blocks[(index + step) % length]
+        done.append(lax.ppermute(sent, axis, [(i, (i + step) % length) for i in range(length)]))
+    blocks = jnp.stack(done)[(index - jnp.arange(length)) % length]
+    return in_order(blocks, concat_dim)
 
 
 def swiglu_rows(rows_in, weights):
@@ -38,7 +61,7 @@
     outgoing = outgoing.reshape(device_count, capacity, model_width)
     count_column = send_counts.astype(jnp.bfloat16).reshape(device_count, 1)
     incoming, arrived = (
-        lax.all_to_all(outgoing, "expert", split_axis=0, concat_axis=0, tiled=True),
+        rotated_exchange(outgoing, "expert", 0, 0),
         lax.all_to_all(count_column, "expert", split_axis=0, concat_axis=0, tiled=True),
     )
     arrived_counts = arrived.reshape(-1).astype(jnp.int32)

time: 307 us -> 342 us (1.11)
  local copies, waits for them, and re-layouts: 56.8 us -> 78.7 us
  waiting for transfers between devices: 157 us -> 168 us
  starting transfers between devices: 36.7 us -> 40.9 us
    all_to_all x1 -> x0, waiting for transfers between devices: 64.7 us -> none  [route_and_run(): lax.all_to_all(outgoing, 'expert', split_axis=0, concat_axis=0, tiled=True)]
    ppermute x0 -> x15, waiting for transfers between devices: none -> 56.6 us  [rotated_exchange(): lax.ppermute(sent, axis, [(i, (i + step) % length) for i in range(length)])]
    all_to_all x1, waiting for transfers between devices: 0.01 us -> 19 us  [route_and_run(): lax.all_to_all(count_column, 'expert', split_axis=0, concat_axis=0, tiled...]
    ppermute x0 -> x15, starting transfers between devices: none -> 17.2 us  [rotated_exchange(): lax.ppermute(sent, axis, [(i, (i + step) % length) for i in range(length)])]
    unnamed x8 -> x22, local copies, waits for them, and re-layouts: 1.31 us -> 16.3 us
    all_to_all x1 -> x0, starting transfers between devices: 6.02 us -> none  [route_and_run(): lax.all_to_all(outgoing, 'expert', split_axis=0, concat_axis=0, tiled=True)]
    all_to_all x1, starting transfers between devices: 24.2 us -> 18.6 us  [route_and_run(): lax.all_to_all(back_slots, 'expert', split_axis=0, concat_axis=0, tiled=T...]
    gather x0 -> x1, local copies, waits for them, and re-layouts: none -> 4.96 us  [rotated_exchange(): blocks = jnp.stack(done)[(index - jnp.arange(length)) % length]]
  transfers between devices with their start and end apart: 3 -> 17, of which waited for: 2 -> 7; matrix products, arithmetic and copies ran while one was open for 13% -> 13% of each run, Pallas kernels for 0% -> 0%
where the time goes in v1:
time: 342 us; the launch traced here: 341 us
  waiting for transfers between devices  168 us (49%)
  local copies, waits for them, and re-layouts  78.7 us (23%)
  starting transfers between devices  40.9 us (12%)
  other arithmetic  32.9 us (10%)
  matrix products  19.3 us (6%)
    all_to_all x1, waiting for transfers between devices, route_and_run(): lax.all_to_all(back_slots, 'expert', split_axis=0, concat_axis=0, tiled=T...  92.4 us
    ppermute x15, waiting for transfers between devices, rotated_exchange(): lax.ppermute(sent, axis, [(i, (i + step) % length) for i in range(length)])  56.6 us
    all_to_all x1, waiting for transfers between devices, route_and_run(): lax.all_to_all(count_column, 'expert', split_axis=0, concat_axis=0, tiled...  19 us
    all_to_all x1, starting transfers between devices, route_and_run(): lax.all_to_all(back_slots, 'expert', split_axis=0, concat_axis=0, tiled=T...  18.6 us
    ppermute x15, starting transfers between devices, rotated_exchange(): lax.ppermute(sent, axis, [(i, (i + step) % length) for i in range(length)])  17.2 us
    unnamed x22, local copies, waits for them, and re-layouts  16.3 us
    gather x7, other arithmetic, route_and_run(): is_live = within < arrived_counts[source_of]  14.4 us
    dot_general x2, matrix products, swiglu_rows(): jnp.dot(hidden, weights[2], preferred_element_type=jnp.float32)  13.1 us
  transfers between devices with their start and end apart: 17, of which 7 were waited for; matrix products, arithmetic and copies ran while one was open for 13% of the time, Pallas kernels for 0%

profile of v1, /device:TPU:15, one launch (start us, length us, event | category | flops | bytes accessed | tf_op | source)
XLA Modules:
  0.0 340.7 jit_solution(8039249460953919788)
XLA Ops:
  0.0 0.8 copy.30
  1.7 1.2 reduce-window.19
  3.4 2.4 scatter_custom_fusion
  6.0 2.4 scatter_custom_fusion.1
  8.5 6.0 %gather_fusion = bf16[1024,2048]{1,0:T(8,128)(2,1)} fusion(bf16[64,2048]{1,0:T(8,128)(2,1)S(1)} %copy-done, s32[1024]{0:T(1024)S(1)} %fusion.20), kind=kCustom, calls=%fused_computation | custom fusion | bytes 8392704 | tf_op jit(solution)/shard_map/gather | solution.py:60
  14.6 2.5 broadcast_select_fusion
  17.1 1.3 dynamic-slice_bitcast_fusion
  18.4 1.8 collective-permute-start
  20.2 1.2 collective-permute-start.1
  21.7 1.0 collective-permute-start.3
  22.7 2.7 collective-permute-start.4
  26.3 5.1 %all-to-all-start = ((bf16[16,1,1]{2,1,0:T(2,128)(2,1)}), bf16[16,1,1]{2,1,0:T(2,128)(2,1)S(1)}, u32[]{:S(2)}, u32[]{:S(2)}) async-start(bf16[16,1,1]{2,1,0:T(2,128)(2,1)} %copy.33), calls=%async_computation | async-start | bytes 16384 | tf_op jit(solution)/shard_map/all_to_all | solution.py:65
  31.5 19.0 %all-to-all-done = bf16[16,1,1]{2,1,0:T(2,128)(2,1)S(1)} async-done(((bf16[16,1,1]{2,1,0:T(2,128)(2,1)}), bf16[16,1,1]{2,1,0:T(2,128)(2,1)S(1)}, u32[]{:S(2)}, u32[]{:S(2)}) %all-to-all-start) | async-done | bytes 64 | tf_op jit(solution)/shard_map/all_to_all | solution.py:65
  51.3 0.9 convert_reduce_fusion.1
  53.0 8.7 %compare_select_fusion.6 = (s32[1024,1]{0,1:T(1,128)S(1)}, s32[1024,1]{0,1:T(1,128)S(1)}) fusion(s32[]{:T(128)} %bitcast.13, s32[]{:T(128)} %bitcast.14, s32[]{:T(128)} %bitcast.15, s32[]{:T(128)} %bitcast.16, s32[]{:T(128)} %bitcast.17, s32[]{:T(128)} %bitcast.19, s32[]{:T(128)} %bitcast.18, s32[]{:T(128)} %bitcast.72, s32[]{:T(128)} %bitcast.71, ...), kind=kLoop, calls=%fused_computation.80 | loop fusion | flops 29696 | bytes 8248 | tf_op jit(solution)/shard_map/gather | solution.py:73
  61.7 5.6 %select_select_fusion = s32[1024]{0:T(1024)S(1)} fusion(pred[1024]{0:T(1024)(128)(4,1)S(1)} %get-tuple-element.110, pred[1024]{0:T(1024)(128)(4,1)S(1)} %get-tuple-element.111, pred[1024]{0:T(1024)(128)(4,1)S(1)} %get-tuple-element.112, pred[1024]{0:T(1024)(128)(4,1)S(1)} %get-tuple-element.113, pred[1024]{0:T(1024)(128)(4,1)S(1)} %get-tuple-element.114, ...), kind=kLoop, calls=%fused_computation.104 | loop fusion | flops 9216 | bytes 17444 | tf_op jit(solution)/shard_map/gather | solution.py:74
  67.3 5.6 %select_select_fusion.1 = s32[1024]{0:T(1024)S(1)} fusion(pred[1024]{0:T(1024)(128)(4,1)S(1)} %get-tuple-element.110, pred[1024]{0:T(1024)(128)(4,1)S(1)} %get-tuple-element.111, pred[1024]{0:T(1024)(128)(4,1)S(1)} %get-tuple-element.112, pred[1024]{0:T(1024)(128)(4,1)S(1)} %get-tuple-element.113, pred[1024]{0:T(1024)(128)(4,1)S(1)} %get-tuple-element.114, ...), kind=kLoop, calls=%fused_computation.105 | loop fusion | flops 9216 | bytes 17444 | tf_op jit(solution)/shard_map/gather | solution.py:73
  72.9 4.3 %scatter_custom_fusion.2 = s32[1024]{0:T(1024)S(1)} fusion(s32[1024]{0:T(1024)S(1)} %bitcast.154, s32[1024]{0:T(1024)S(1)} %iota.51, s32[]{:T(128)} %constant.186.clone.1), kind=kCustom, calls=%fused_computation.116 | custom fusion | bytes 4100 | tf_op jit(solution)/shard_map/scatter | solution.py:77
  78.0 2.7 collective-permute-start.5
  80.7 1.7 bitcast_dynamic-update-slice_fusion.14
  82.4 1.4 collective-permute-start.6
  83.9 1.7 bitcast_dynamic-update-slice_fusion.13
  85.5 1.5 collective-permute-start.7
  87.0 1.7 bitcast_dynamic-update-slice_fusion.12
  89.3 1.7 bitcast_dynamic-update-slice_fusion.11
  90.9 1.4 collective-permute-start.9
  92.4 1.7 bitcast_dynamic-update-slice_fusion.10
  94.0 26.1 %collective-permute-done.5 = bf16[1,64,2048]{2,1,0:T(8,128)(2,1)S(1)} collective-permute-done((bf16[1,64,2048]{2,1,0:T(8,128)(2,1)S(1)}, bf16[1,64,2048]{2,1,0:T(8,128)(2,1)S(1)}, u32[]{:S(2)}, u32[]{:S(2)}) %collective-permute-start.5) | collective-permute-done | bytes 262176 | tf_op jit(solution)/shard_map/ppermute | solution.py:27
  120.9 4.9 %collective-permute-done.6 = bf16[1,64,2048]{2,1,0:T(8,128)(2,1)S(1)} collective-permute-done((bf16[1,64,2048]{2,1,0:T(8,128)(2,1)S(1)}, bf16[1,64,2048]{2,1,0:T(8,128)(2,1)S(1)}, u32[]{:S(2)}, u32[]{:S(2)}) %collective-permute-start.6) | collective-permute-done | bytes 262176 | tf_op jit(solution)/shard_map/ppermute | solution.py:27
  126.5 10.5 %collective-permute-done.7 = bf16[1,64,2048]{2,1,0:T(8,128)(2,1)S(1)} collective-permute-done((bf16[1,64,2048]{2,1,0:T(8,128)(2,1)S(1)}, bf16[1,64,2048]{2,1,0:T(8,128)(2,1)S(1)}, u32[]{:S(2)}, u32[]{:S(2)}) %collective-permute-start.7) | collective-permute-done | bytes 262176 | tf_op jit(solution)/shard_map/ppermute | solution.py:27
  138.5 2.5 collective-permute-start.14
  143.2 0.9 collective-permute-done.12
  144.8 14.2 %collective-permute-done.13 = bf16[1,64,2048]{2,1,0:T(8,128)(2,1)S(1)} collective-permute-done((bf16[1,64,2048]{2,1,0:T(8,128)(2,1)S(1)}, bf16[1,64,2048]{2,1,0:T(8,128)(2,1)S(1)}, u32[]{:S(2)}, u32[]{:S(2)}) %collective-permute-start.13) | collective-permute-done | bytes 262176 | tf_op jit(solution)/shard_map/ppermute | solution.py:27
  160.4 5.0 %gather_fusion.1 = bf16[16,64,2048]{2,1,0:T(8,128)(2,1)} fusion(bf16[16,64,2048]{2,1,0:T(8,128)(2,1)} %bitcast.143, s32[1024]{0:T(1024)S(1)} %pad_clamp_fusion.1), kind=kCustom, calls=%fused_computation.1 | custom fusion | bytes 8388672 | tf_op jit(solution)/shard_map/gather | solution.py:28
  165.4 4.7 %concatenate.3 = bf16[1025,2048]{1,0:T(8,128)(2,1)} pad(bf16[1024,2048]{1,0:T(8,128)(2,1)} %bitcast.142, bf16[]{:T(256)} %constant.190.clone.1), padding=0_1x0_0 | pad | bytes 8392706 | tf_op jit(solution)/shard_map/concatenate | solution.py:79
  170.1 11.6 %gather_fusion.2 = bf16[1024,2048]{1,0:T(8,128)(2,1)} fusion(bf16[1025,2048]{1,0:T(8,128)(2,1)} %concatenate.3, s32[1024]{0:T(1024)S(1)} %fusion.21), kind=kCustom, calls=%fused_computation.2 | custom fusion | bytes 8392704 | tf_op jit(solution)/shard_map/gather | solution.py:83
  181.7 2.4 broadcast_in_dim.63
  184.6 19.3 %while.10 = (s32[]{:T(128)}, bf16[1024,2048]{1,0:T(8,128)(2,1)}, s32[]{:T(128)}, bf16[1024,2048]{1,0:T(8,128)(2,1)}, bf16[2048,768]{1,0:T(8,128)(2,1)S(1)}, /*in...) while((s32[]{:T(128)}, bf16[1024,2048]{1,0:T(8,128)(2,1)}, ...), condition=%wide.region_10.11_spmd, body=%wide.region_9.10_spmd.sunk | while | flops 2417623040 | bytes 14156959 | solution.py:46
  184.6 3.1 fusion.52
  187.7 6.5 %fusion.53 = bf16[1024,2048]{1,0:T(8,128)(2,1)} fusion(bf16[1024,2048]{1,0:T(8,128)(2,1)} %get-tuple-element.176, s32[]{:T(128)S(6)} %select_n.414, bf16[768,2048]{1,0:T(8,128)(2,1)} %get-tuple-element.192, bf16[2048,768]{1,0:T(8,128)(2,1)} %get-tuple-element.191, bf16[1024,2048]{1,0:T(8,128)(2,1)} %get-tuple-element.189, f32[256,768]{1,0:T(8,128)} %fusion.52), kind=kOutput, calls=%fused_computation.9.clone.1 | convolution fusion | flops 1612316672 | bytes 9176064 | tf_op jit(solution)/shard_map/while/body/dot_general | solution.py:36
  194.2 3.1 fusion.52
  197.4 6.6 %fusion.53 = bf16[1024,2048]{1,0:T(8,128)(2,1)} fusion(bf16[1024,2048]{1,0:T(8,128)(2,1)} %get-tuple-element.176, s32[]{:T(128)S(6)} %select_n.414, bf16[768,2048]{1,0:T(8,128)(2,1)} %get-tuple-element.192, bf16[2048,768]{1,0:T(8,128)(2,1)} %get-tuple-element.191, bf16[1024,2048]{1,0:T(8,128)(2,1)} %get-tuple-element.189, f32[256,768]{1,0:T(8,128)} %fusion.52), kind=kOutput, calls=%fused_computation.9.clone.1 | convolution fusion | flops 1612316672 | bytes 9176064 | tf_op jit(solution)/shard_map/while/body/dot_general | solution.py:36
  203.9 11.6 %gather_fusion.3 = bf16[1024,2048]{1,0:T(8,128)(2,1)} fusion(bf16[1024,2048]{1,0:T(8,128)(2,1)} %get-tuple-element.43, s32[1024]{0:T(1024)S(1)} %broadcast_clamp_fusion), kind=kCustom, calls=%fused_computation.3 | custom fusion | bytes 8392704 | tf_op jit(solution)/shard_map/gather | solution.py:88
  215.5 4.5 %broadcast_select_fusion.1 = bf16[16,64,2048]{2,1,0:T(8,128)(2,1)} fusion(bf16[16,64,2048]{2,1,0:T(8,128)(2,1)} %bitcast.140, pred[16,64]{1,0:T(8,128)(4,1)S(1)} %fusion.16), kind=kLoop, calls=%fused_computation.22 | loop fusion | flops 2097152 | bytes 8389632 | tf_op jit(solution)/shard_map/jit(_where)/select_n | solution.py:89
  219.9 18.6 %all-to-all-start.1 = ((bf16[16,64,2048]{2,1,0:T(8,128)(2,1)}), bf16[16,64,2048]{2,1,0:T(8,128)(2,1)}, u32[]{:S(2)}, u32[]{:S(2)}) async-start(bf16[16,64,2048]{2,1,0:T(8,128)(2,1)} %broadcast_select_fusion.1), calls=%async_computation.1 | async-start | bytes 8388608 | tf_op jit(solution)/shard_map/all_to_all | solution.py:91
  238.7 92.4 %all-to-all-done.1 = bf16[16,64,2048]{2,1,0:T(8,128)(2,1)} async-done(((bf16[16,64,2048]{2,1,0:T(8,128)(2,1)}), bf16[16,64,2048]{2,1,0:T(8,128)(2,1)}, u32[]{:S(2)}, u32[]{:S(2)}) %all-to-all-start.1) | async-done | bytes 4194336 | tf_op jit(solution)/shard_map/all_to_all | solution.py:91
  331.0 7.1 %gather_fusion.4 = bf16[512,2048]{1,0:T(8,128)(2,1)S(1)} fusion(bf16[1024,2048]{1,0:T(8,128)(2,1)} %bitcast.81, s32[1024]{0:T(1024)S(1)} %pad_clamp_fusion), kind=kCustom, calls=%fused_computation.4 | custom fusion | bytes 4196352 | tf_op jit(solution)/shard_map/gather | solution.py:92
  338.2 2.5 fusion.12
  (74 shorter events, 13.0 us)
Async XLA Ops:
  0.0 8.5 %copy-start = (bf16[64,2048]{1,0:T(8,128)(2,1)S(1)}, bf16[64,2048]{1,0:T(8,128)(2,1)}, u32[]{:S(2)}) copy-start(bf16[64,2048]{1,0:T(8,128)(2,1)} %param.8) | copy-start | bytes 786436
  18.4 59.6 %collective-permute-start = (bf16[1,64,2048]{2,1,0:T(8,128)(2,1)}, bf16[1,64,2048]{2,1,0:T(8,128)(2,1)}, u32[]{:S(2)}, u32[]{:S(2)}) collective-permute-start(bf16[1,64,2048]{2,1,0:T(8,128)(2,1)} %get-tuple-element.74), channel_id=1, source_target_pairs={{0,1},{1,2},{2,3},{3,4},{4,5},{5,6},{6,7},{7,8},{8,9},{9,10},{10,1... | collective-permute-start | bytes 786440 | tf_op jit(solution)/shard_map/ppermute | solution.py:27
  20.2 62.2 %collective-permute-start.1 = (bf16[1,64,2048]{2,1,0:T(8,128)(2,1)}, bf16[1,64,2048]{2,1,0:T(8,128)(2,1)}, u32[]{:S(2)}, u32[]{:S(2)}) collective-permute-start(bf16[1,64,2048]{2,1,0:T(8,128)(2,1)} %get-tuple-element.73), channel_id=1, source_target_pairs={{0,2},{1,3},{2,4},{3,5},{4,6},{5,7},{6,8},{7,9},{8,10},{9,11},{10,... | collective-permute-start | bytes 786440 | tf_op jit(solution)/shard_map/ppermute | solution.py:27
  21.4 64.1 %collective-permute-start.2 = (bf16[1,64,2048]{2,1,0:T(8,128)(2,1)}, bf16[1,64,2048]{2,1,0:T(8,128)(2,1)}, u32[]{:S(2)}, u32[]{:S(2)}) collective-permute-start(bf16[1,64,2048]{2,1,0:T(8,128)(2,1)} %get-tuple-element.72), channel_id=1, source_target_pairs={{0,3},{1,4},{2,5},{3,6},{4,7},{5,8},{6,9},{7,10},{8,11},{9,12},{10... | collective-permute-start | bytes 786440 | tf_op jit(solution)/shard_map/ppermute | solution.py:27
  21.7 66.9 %collective-permute-start.3 = (bf16[1,64,2048]{2,1,0:T(8,128)(2,1)S(1)}, bf16[1,64,2048]{2,1,0:T(8,128)(2,1)}, u32[]{:S(2)}, u32[]{:S(2)}) collective-permute-start(bf16[1,64,2048]{2,1,0:T(8,128)(2,1)S(1)} %get-tuple-element.71), channel_id=1, source_target_pairs={{0,4},{1,5},{2,6},{3,7},{4,8},{5,9},{6,10},{7,11},{8,12},{9,13},{1... | collective-permute-start | bytes 786440 | tf_op jit(solution)/shard_map/ppermute | solution.py:27
  22.7 68.2 %collective-permute-start.4 = (bf16[1,64,2048]{2,1,0:T(8,128)(2,1)S(1)}, bf16[1,64,2048]{2,1,0:T(8,128)(2,1)}, u32[]{:S(2)}, u32[]{:S(2)}) collective-permute-start(bf16[1,64,2048]{2,1,0:T(8,128)(2,1)S(1)} %get-tuple-element.70), channel_id=1, source_target_pairs={{0,5},{1,6},{2,7},{3,8},{4,9},{5,10},{6,11},{7,12},{8,13},{9,14},{... | collective-permute-start | bytes 786440 | tf_op jit(solution)/shard_map/ppermute | solution.py:27
  26.3 24.2 %all-to-all-start = ((bf16[16,1,1]{2,1,0:T(2,128)(2,1)}), bf16[16,1,1]{2,1,0:T(2,128)(2,1)S(1)}, u32[]{:S(2)}, u32[]{:S(2)}) async-start(bf16[16,1,1]{2,1,0:T(2,128)(2,1)} %copy.33), calls=%async_computation | async-start | bytes 16384 | tf_op jit(solution)/shard_map/all_to_all | solution.py:65
  78.0 42.1 %collective-permute-start.5 = (bf16[1,64,2048]{2,1,0:T(8,128)(2,1)S(1)}, bf16[1,64,2048]{2,1,0:T(8,128)(2,1)S(1)}, u32[]{:S(2)}, u32[]{:S(2)}) collective-permute-start(bf16[1,64,2048]{2,1,0:T(8,128)(2,1)S(1)} %get-tuple-element.69), channel_id=1, source_target_pairs={{0,6},{1,7},{2,8},{3,9},{4,10},{5,11},{6,12},{7,13},{8,14},{9,15},... | collective-permute-start | bytes 786440 | tf_op jit(solution)/shard_map/ppermute | solution.py:27
  82.4 43.3 %collective-permute-start.6 = (bf16[1,64,2048]{2,1,0:T(8,128)(2,1)S(1)}, bf16[1,64,2048]{2,1,0:T(8,128)(2,1)S(1)}, u32[]{:S(2)}, u32[]{:S(2)}) collective-permute-start(bf16[1,64,2048]{2,1,0:T(8,128)(2,1)S(1)} %get-tuple-element.68), channel_id=1, source_target_pairs={{0,7},{1,8},{2,9},{3,10},{4,11},{5,12},{6,13},{7,14},{8,15},{9,0},... | collective-permute-start | bytes 786440 | tf_op jit(solution)/shard_map/ppermute | solution.py:27
  85.5 51.5 %collective-permute-start.7 = (bf16[1,64,2048]{2,1,0:T(8,128)(2,1)S(1)}, bf16[1,64,2048]{2,1,0:T(8,128)(2,1)S(1)}, u32[]{:S(2)}, u32[]{:S(2)}) collective-permute-start(bf16[1,64,2048]{2,1,0:T(8,128)(2,1)S(1)} %get-tuple-element.67), channel_id=1, source_target_pairs={{0,8},{1,9},{2,10},{3,11},{4,12},{5,13},{6,14},{7,15},{8,0},{9,1},... | collective-permute-start | bytes 786440 | tf_op jit(solution)/shard_map/ppermute | solution.py:27
  88.7 49.0 %collective-permute-start.8 = (bf16[1,64,2048]{2,1,0:T(8,128)(2,1)S(1)}, bf16[1,64,2048]{2,1,0:T(8,128)(2,1)S(1)}, u32[]{:S(2)}, u32[]{:S(2)}) collective-permute-start(bf16[1,64,2048]{2,1,0:T(8,128)(2,1)S(1)} %get-tuple-element.66), channel_id=1, source_target_pairs={{0,9},{1,10},{2,11},{3,12},{4,13},{5,14},{6,15},{7,0},{8,1},{9,2},... | collective-permute-start | bytes 786440 | tf_op jit(solution)/shard_map/ppermute | solution.py:27
  90.9 47.5 %collective-permute-start.9 = (bf16[1,64,2048]{2,1,0:T(8,128)(2,1)S(1)}, bf16[1,64,2048]{2,1,0:T(8,128)(2,1)S(1)}, u32[]{:S(2)}, u32[]{:S(2)}) collective-permute-start(bf16[1,64,2048]{2,1,0:T(8,128)(2,1)S(1)} %get-tuple-element.65), channel_id=1, source_target_pairs={{0,10},{1,11},{2,12},{3,13},{4,14},{5,15},{6,0},{7,1},{8,2},{9,3},... | collective-permute-start | bytes 786440 | tf_op jit(solution)/shard_map/ppermute | solution.py:27
  120.1 21.6 %collective-permute-start.10 = (bf16[1,64,2048]{2,1,0:T(8,128)(2,1)S(1)}, bf16[1,64,2048]{2,1,0:T(8,128)(2,1)S(1)}, u32[]{:S(2)}, u32[]{:S(2)}) collective-permute-start(bf16[1,64,2048]{2,1,0:T(8,128)(2,1)S(1)} %get-tuple-element.64), channel_id=1, source_target_pairs={{0,11},{1,12},{2,13},{3,14},{4,15},{5,0},{6,1},{7,2},{8,3},{9,4},{... | collective-permute-start | bytes 786440 | tf_op jit(solution)/shard_map/ppermute | solution.py:27
  125.8 16.7 %collective-permute-start.11 = (bf16[1,64,2048]{2,1,0:T(8,128)(2,1)S(1)}, bf16[1,64,2048]{2,1,0:T(8,128)(2,1)S(1)}, u32[]{:S(2)}, u32[]{:S(2)}) collective-permute-start(bf16[1,64,2048]{2,1,0:T(8,128)(2,1)S(1)} %get-tuple-element.63), channel_id=1, source_target_pairs={{0,12},{1,13},{2,14},{3,15},{4,0},{5,1},{6,2},{7,3},{8,4},{9,5},{1... | collective-permute-start | bytes 786440 | tf_op jit(solution)/shard_map/ppermute | solution.py:27
  137.0 7.1 %collective-permute-start.12 = (bf16[1,64,2048]{2,1,0:T(8,128)(2,1)S(1)}, bf16[1,64,2048]{2,1,0:T(8,128)(2,1)S(1)}, u32[]{:S(2)}, u32[]{:S(2)}) collective-permute-start(bf16[1,64,2048]{2,1,0:T(8,128)(2,1)S(1)} %get-tuple-element.62), channel_id=1, source_target_pairs={{0,13},{1,14},{2,15},{3,0},{4,1},{5,2},{6,3},{7,4},{8,5},{9,6},{10... | collective-permute-start | bytes 786440 | tf_op jit(solution)/shard_map/ppermute | solution.py:27
  137.7 21.2 %collective-permute-start.13 = (bf16[1,64,2048]{2,1,0:T(8,128)(2,1)S(1)}, bf16[1,64,2048]{2,1,0:T(8,128)(2,1)S(1)}, u32[]{:S(2)}, u32[]{:S(2)}) collective-permute-start(bf16[1,64,2048]{2,1,0:T(8,128)(2,1)S(1)} %get-tuple-element.61), channel_id=1, source_target_pairs={{0,14},{1,15},{2,0},{3,1},{4,2},{5,3},{6,4},{7,5},{8,6},{9,7},{10,... | collective-permute-start | bytes 786440 | tf_op jit(solution)/shard_map/ppermute | solution.py:27
  138.5 21.2 %collective-permute-start.14 = (bf16[1,64,2048]{2,1,0:T(8,128)(2,1)S(1)}, bf16[1,64,2048]{2,1,0:T(8,128)(2,1)S(1)}, u32[]{:S(2)}, u32[]{:S(2)}) collective-permute-start(bf16[1,64,2048]{2,1,0:T(8,128)(2,1)S(1)} %get-tuple-element.60), channel_id=1, source_target_pairs={{0,15},{1,0},{2,1},{3,2},{4,3},{5,4},{6,5},{7,6},{8,7},{9,8},{10,9... | collective-permute-start | bytes 786440 | tf_op jit(solution)/shard_map/ppermute | solution.py:27
  181.7 2.9 copy-start.2
  219.9 18.6 %copy-start.1 = (f32[64,8]{0,1:T(8,128)S(1)}, f32[64,8]{0,1:T(8,128)}, u32[]{:S(2)}) copy-start(f32[64,8]{0,1:T(8,128)} %param.10) | copy-start | bytes 6148
  219.9 111.1 %all-to-all-start.1 = ((bf16[16,64,2048]{2,1,0:T(8,128)(2,1)}), bf16[16,64,2048]{2,1,0:T(8,128)(2,1)}, u32[]{:S(2)}, u32[]{:S(2)}) async-start(bf16[16,64,2048]{2,1,0:T(8,128)(2,1)} %broadcast_select_fusion.1), calls=%async_computation.1 | async-start | bytes 8388608 | tf_op jit(solution)/shard_map/all_to_all | solution.py:91
